TPU v7x, 32 devices: a whole 2x2x4 slice. The times are simulated.
32 devices in a mesh: gx: 4 (over z), gy: 8 (over y, x, core).
Axes of the slice: x: 2, y: 2, z: 4, core: 2. Of those that a mesh axis runs over, the one named last changes fastest.
Arguments:
- point_feats: bfloat16 [512, 64, 128], P(('gx', 'gy')), may hold values from -6 to 6
- offsets: bfloat16 [512, 3, 128], P(('gx', 'gy')), may hold values from 0 to 1
- targets: int32 [512, 1], P(('gx', 'gy')), may hold values from 0 to 7; in each aligned block of 16 rows (0 to 15, 16 to 31, ...) at most 4 rows name the same one
- zstart: int32 [512], P(('gx', 'gy')), may hold values from 0 to 63
- enc_in: float32 [3, 64], replicated, may hold values from -4 to 4
- enc_bias: float32 [64], replicated, may hold values from -4 to 4
- enc_out: bfloat16 [64, 64], replicated, may hold values from -0.75 to 0.75
- dec_in: float32 [3, 64], replicated, may hold values from -4 to 4
- dec_bias: float32 [64], replicated, may hold values from -4 to 4
- dec_out: bfloat16 [64, 64], replicated, may hold values from -0.75 to 0.75
- spec_weight: float32 [32, 32, 32, 4096], P(None, 'gx', 'gy'), may hold values from -0.75 to 0.75
- local_weight: float32 [64, 64], replicated, may hold values from -0.75 to 0.75
- local_bias: float32 [64], replicated, may hold values from -3 to 3
- head_weight: float32 [64], replicated, may hold values from -4 to 4
Outputs:
- pressure: float32 [512, 128], P(('gx', 'gy'))
Inputs may be any that keep to these rules, and one draw needn't show every extreme that they name: `targets`: A block's cells lie in the pencil of its own gx row with this gy index; at most 4 blocks of one device share a target, and exactly 4 do on some devices.
All inputs are finite; a program needn't handle non-finite values.
Results may differ from a plain program's by a relative error of at most 0.0014.
Values may be sent and summed in bfloat16 or wider, within the bound.
No kernel may reach another device: no remote copies, remote signals or barrier semaphores. Data moves between devices by JAX's collectives and lax.ppermute only.
A program may use at most 128 MiB of HBM per device.

v0:
```python
import jax
import jax.numpy as jnp
from jax import lax
from jax.sharding import PartitionSpec as P

G = 64
M = 32
kernel_spread = 2.0
highest = lax.Precision.HIGHEST


def real_basis(length, modes):
    half = modes // 2
    places = jnp.arange(length).astype(jnp.float32)
    frequency = jnp.arange(half).astype(jnp.float32)
    angle_cos = 2.0 * jnp.pi * frequency[:, None] * places[None, :] / length
    angle_sin = 2.0 * jnp.pi * (frequency[:, None] + 1.0) * places[None, :] / length
    table = jnp.concatenate([jnp.cos(angle_cos), jnp.sin(angle_sin)], 0)
    return table * jnp.float32((2.0 / length) ** 0.5)


def tile_terms(offset_rows, weight_in, bias_in, cells_x, cells_y):
    offset_rows = offset_rows.astype(jnp.float32)
    cell_ids = jnp.arange(cells_x * cells_y)
    center_x = (cell_ids // cells_y).astype(jnp.float32) + 0.5
    center_y = (cell_ids % cells_y).astype(jnp.float32) + 0.5
    delta_x = (center_x[None, :, None] - cells_x * offset_rows[:, 0][:, None, :]) / kernel_spread
    delta_y = (center_y[None, :, None] - cells_y * offset_rows[:, 1][:, None, :]) / kernel_spread
    delta_z = (0.5 - offset_rows[:, 2][:, None, :]) / kernel_spread
    closeness = jnp.exp(-0.5 * (delta_x * delta_x + delta_y * delta_y + delta_z * delta_z))
    before = (
        delta_x[..., None] * weight_in[0]
        + delta_y[..., None] * weight_in[1]
        + delta_z[..., None] * weight_in[2]
        + bias_in
    )
    return (jax.nn.gelu(before, approximate=False) * closeness[..., None]).astype(jnp.bfloat16)


def encode(weighted, feats, out_weight):
    partial_sums = jnp.einsum("bcph,bop->bcho", weighted, feats, preferred_element_type=jnp.float32)
    return jnp.einsum(
        "bcho,ho->boc", partial_sums, out_weight.astype(jnp.float32), precision=highest
    ) * feats.shape[2] ** (-0.5)


def decode(weighted, tile_values, out_weight):
    folded = (
        out_weight.astype(jnp.float32)[None, None, :, :]
        * jnp.transpose(tile_values.astype(jnp.float32), (0, 2, 1))[:, :, None, :]
    ).astype(jnp.bfloat16)
    return jnp.einsum(
        "bcph,bcho->bop", weighted, folded, preferred_element_type=jnp.float32
    ) * weighted.shape[1] ** (-0.5)


def run_groups(function, arrays, row_count):
    group_size = 8
    shaped = tuple(
        (
            member.reshape((row_count // group_size, group_size) + member.shape[1:])
            for member in arrays
        )
    )
    result = lax.map(function, shaped)
    return result.reshape((row_count,) + result.shape[2:])


def fourier(pencil, spec_weight, local_weight, local_bias, table):
    channels = pencil.shape[0]
    spectrum = jnp.einsum("oxyz,kz->oxyk", pencil, table, precision=highest)
    spectrum = lax.all_to_all(
        spectrum.astype(jnp.bfloat16), "gy", split_axis=3, concat_axis=2, tiled=True
    ).astype(spectrum.dtype)
    spectrum = jnp.einsum("oxyk,ly->oxlk", spectrum, table, precision=highest)
    spectrum = lax.all_to_all(spectrum, "gx", split_axis=2, concat_axis=1, tiled=True)
    spectrum = jnp.einsum("oxlk,jx->ojlk", spectrum, table, precision=highest)
    mode_weight = spec_weight.reshape(spec_weight.shape[:3] + (channels, channels))
    mixed_modes = jnp.einsum("ojlk,jlkoq->qjlk", spectrum, mode_weight, precision=highest)
    returned = jnp.einsum("ojlk,jx->oxlk", mixed_modes, table, precision=highest)
    returned = lax.all_to_all(
        returned.astype(jnp.bfloat16), "gx", split_axis=1, concat_axis=2, tiled=True
    ).astype(returned.dtype)
    returned = jnp.einsum("oxlk,ly->oxyk", returned, table, precision=highest)
    returned = lax.all_to_all(
        returned.astype(jnp.bfloat16), "gy", split_axis=2, concat_axis=3, tiled=True
    ).astype(returned.dtype)
    returned = jnp.einsum("oxyk,kz->oxyz", returned, table, precision=highest)
    local_term = (
        jnp.einsum("oxyz,oq->qxyz", pencil, local_weight, precision=highest)
        + local_bias[:, None, None, None]
    )
    return jax.nn.gelu(returned + local_term, approximate=False).astype(jnp.bfloat16)


def local(
    point_feats,
    offsets,
    targets,
    zstart,
    enc_in,
    enc_bias,
    enc_out,
    dec_in,
    dec_bias,
    dec_out,
    spec_weight,
    local_weight,
    local_bias,
    head_weight,
):
    rows_count = lax.axis_size("gx")
    cols_count = lax.axis_size("gy")
    cells_x = G // rows_count
    cells_y = G // cols_count
    tile_cells = cells_x * cells_y
    block_count = point_feats.shape[0]
    channels = point_feats.shape[1]
    capacity = max(2, 2 * block_count // cols_count)
    slot_count = cols_count * capacity
    target = targets[:, 0]
    onehot = (target[:, None] == jnp.arange(cols_count)[None, :]).astype(jnp.int32)
    slot_rank = jnp.sum(onehot * (jnp.cumsum(onehot, axis=0) - onehot), axis=1)
    slot_of = target * capacity + slot_rank
    placement = jnp.arange(slot_count)[:, None] == slot_of[None, :]
    place_float = placement.astype(jnp.float32)
    place_half = placement.astype(jnp.bfloat16)
    planes_sent = jnp.dot(place_float, zstart.astype(jnp.float32), precision=highest)
    table = real_basis(G, M)

    def encode_rows(pieces):
        feats_group, offs_group = pieces
        weighted = tile_terms(offs_group, enc_in, enc_bias, cells_x, cells_y)
        return encode(weighted, feats_group, enc_out)

    def decode_rows(pieces):
        tiles_group, offs_group = pieces
        weighted = tile_terms(offs_group, dec_in, dec_bias, cells_x, cells_y)
        values = decode(weighted, tiles_group, dec_out)
        return jnp.einsum(
            "bop,o->bp", jax.nn.gelu(values, approximate=False), head_weight, precision=highest
        )

    own_terms = run_groups(encode_rows, (point_feats, offsets), block_count)
    send_terms = jnp.einsum("sb,boc->soc", place_float, own_terms, precision=highest)
    got_terms, got_planes = (
        lax.all_to_all(
            send_terms.reshape(cols_count, capacity, channels, tile_cells),
            "gy",
            split_axis=0,
            concat_axis=0,
            tiled=True,
        ),
        lax.all_to_all(
            planes_sent.reshape(cols_count, capacity), "gy", split_axis=0, concat_axis=0, tiled=True
        ),
    )
    contrib = got_terms.reshape(slot_count, channels, tile_cells)
    planes_got = got_planes.reshape(slot_count)
    plane_table = planes_got[:, None] == jnp.arange(G).astype(jnp.float32)[None, :]
    pencil = jnp.einsum("soc,sz->ocz", contrib, plane_table.astype(jnp.float32), precision=highest)
    pencil = pencil.reshape(channels, cells_x, cells_y, G)
    latent = fourier(pencil, spec_weight, local_weight, local_bias, table).reshape(
        channels, tile_cells, G
    )
    tile_values = jnp.einsum(
        "ocz,sz->soc", latent, plane_table.astype(jnp.bfloat16), preferred_element_type=jnp.float32
    ).astype(jnp.bfloat16)
    returned = lax.all_to_all(
        tile_values.reshape(cols_count, capacity, channels, tile_cells),
        "gy",
        split_axis=0,
        concat_axis=0,
        tiled=True,
    )
    returned = returned.reshape(slot_count, channels, tile_cells)
    own_tiles = jnp.einsum(
        "sb,soc->boc", place_half, returned, preferred_element_type=jnp.float32
    ).astype(jnp.bfloat16)
    return run_groups(decode_rows, (own_tiles, offsets), block_count)


def solution(mesh):
    placed = (
        P(("gx", "gy"), None, None),
        P(("gx", "gy"), None, None),
        P(("gx", "gy"), None),
        P(("gx", "gy")),
        P(),
        P(),
        P(),
        P(),
        P(),
        P(),
        P(None, "gx", "gy", None),
        P(),
        P(),
        P(),
    )
    return jax.shard_map(
        local, mesh=mesh, in_specs=placed, out_specs=P(("gx", "gy"), None), check_vma=False
    )
```

profile of v0, /device:TPU:0, one launch (start us, length us, event | category | flops | bytes accessed | tf_op | source)
XLA Modules:
  0.0 560.5 jit_solution(12473694886595939378)
XLA Ops:
  0.8 0.8 select_reduce_fusion
  2.8 0.8 convolution_bitcast_fusion.2
  4.4 5.2 all-to-all-start
  10.1 1.3 copy.59
  11.5 179.2 %while.24 = (s32[]{:T(128)}, f32[2,8,64,128]{3,2,1,0:T(8,128)}, bf16[2,8,3,128]{3,1,2,0:T(8,128)(2,1)}, f32[3,64]{1,0:T(4,128)}, f32[64]{0:T(128)}, /*index=5*/b...) while((s32[]{:T(128)}, f32[2,8,64,128]{3,2,1,0:T(8,128)}, bf16[2,8,3,128]{3,1,2,0:T(8,128)(2,1)}, ...), condition=%wide.region_3.4_spmd, body=%wide.region_2.3_spmd.sunk | while | flops 1678981120 | bytes 9416085 | solution.py:65
  12.5 0.8 slice_bitcast_fusion.8
  14.1 85.9 %multiply_reduce_fusion.2 = f32[64,8,128]{0,2,1:T(8,128)S(1)} fusion(f32[64,64]{0,1:T(8,128)S(1)} %bitcast_convert_fusion.6, f32[8,128,128]{2,1,0:T(8,128)S(1)} %get-tuple-element.435, f32[64]{0:T(128)} %get-tuple-element.482, f32[8,128,64]{1,2,0:T(8,128)S(1)} %broadcast_multiply_fusion.4, f32[64]{0:T(128)S(1)} %get-tuple-element.438, ...), kind=kOutput, calls=%fused_computation.219.clone.3 | convolution fusion | flops 1677656064 | bytes 2246144 | tf_op jit(solution)/shard_map/while/body/eval_jaxpr/bcph,bop->bcho/dot_general | solution.py:41
  102.0 0.8 slice_bitcast_fusion.8
  103.6 85.9 %multiply_reduce_fusion.2 = f32[64,8,128]{0,2,1:T(8,128)S(1)} fusion(f32[64,64]{0,1:T(8,128)S(1)} %bitcast_convert_fusion.6, f32[8,128,128]{2,1,0:T(8,128)S(1)} %get-tuple-element.435, f32[64]{0:T(128)} %get-tuple-element.482, f32[8,128,64]{1,2,0:T(8,128)S(1)} %broadcast_multiply_fusion.4, f32[64]{0:T(128)S(1)} %get-tuple-element.438, ...), kind=kOutput, calls=%fused_computation.219.clone.3 | convolution fusion | flops 1677656064 | bytes 2246144 | tf_op jit(solution)/shard_map/while/body/eval_jaxpr/bcph,bop->bcho/dot_general | solution.py:41
  190.7 1.8 fusion.300
  192.5 1.2 copy.61
  193.7 4.2 all-to-all-start.1
  198.6 1.3 reduce.5
  200.0 13.3 %all-to-all-done.1 = f32[8,4,64,128]{3,2,1,0:T(8,128)S(1)} async-done(((f32[8,4,64,128]{3,2,1,0:T(8,128)}), f32[8,4,64,128]{3,2,1,0:T(8,128)S(1)}, u32[]{:S(2)}, u32[]{:S(2)}) %all-to-all-start.1) | async-done | bytes 1048608 | tf_op jit(solution)/shard_map/all_to_all | solution.py:147
  213.3 1.8 copy.62
  215.1 3.5 fusion.309
  218.7 2.1 copy-done.1
  220.7 11.4 %convolution_convert_fusion.1 = bf16[64,16,8,32]{0,3,2,1:T(8,128)(2,1)S(1)} fusion(f32[64,16,8,64]{3,0,2,1:T(8,128)S(1)} %fusion.309, f32[16,64]{1,0:T(8,128)S(1)} %get-tuple-element.319, f32[16,64]{1,0:T(8,128)S(1)} %get-tuple-element.318), kind=kOutput, calls=%fused_computation.359 | convolution fusion | flops 201592832 | bytes 2629632 | tf_op jit(solution)/shard_map/oxyz,kz->oxyk/dot_general | solution.py:71
  232.6 0.9 reshape.239
  233.5 12.1 %all_to_all.91 = bf16[8,2,16384]{2,1,0:T(2,128)(2,1)S(1)} all-to-all(bf16[8,2,16384]{2,1,0:T(2,128)(2,1)S(1)} %reshape.239), channel_id=1, replica_groups=mesh['gx'=4,'gy'=8] {'gy'}, dimensions={0} | all-to-all | bytes 1048576 | tf_op jit(solution)/shard_map/all_to_all | solution.py:72
  247.6 1.8 reshape.241
  249.3 4.9 all-to-all-start.3
  254.3 28.9 %reshape.204 = f32[32,8,4,64,64]{4,3,2,1,0:T(8,128)} reshape(f32[32,8,4,4096]{3,2,1,0:T(4,128)} %param.28) | data formatting | bytes 33554432 | tf_op jit(solution)/shard_map/reshape | solution.py:78
  283.7 2.1 reduce.8
  287.3 1.2 convolution_bitcast_fusion.1
  288.5 32.6 %fusion.303 = f32[32,8,4,1,64]{4,3,2,1,0:T(1,128)S(1)} fusion(f32[32,8,4,64,64]{4,3,2,1,0:T(8,128)} %reshape.204, f32[64,32,8,4,1]{0,1,3,2,4:T(8,128)S(1)} %convolution_bitcast_fusion.1), kind=kOutput, calls=%fused_computation.378 | convolution fusion | flops 50331648 | bytes 17301504 | tf_op jit(solution)/shard_map/ojlk,jlkoq->qjlk/dot_general | solution.py:79
  321.2 1.2 fusion.293
  323.2 12.7 %all_to_all.92 = bf16[4,2,16384]{2,1,0:T(2,128)(2,1)S(1)} all-to-all(bf16[4,2,16384]{2,1,0:T(2,128)(2,1)S(1)} %reshape.243), channel_id=1, replica_groups=mesh['gx'=4,'gy'=8] {'gx'}, dimensions={0} | all-to-all | bytes 524288 | tf_op jit(solution)/shard_map/all_to_all | solution.py:81
  336.3 1.0 fusion.289
  337.4 0.8 copy.138
  338.9 12.3 %all_to_all.93 = bf16[8,2,16384]{2,1,0:T(2,128)(2,1)S(1)} all-to-all(bf16[8,2,16384]{2,1,0:T(2,128)(2,1)S(1)} %reshape.245), channel_id=1, replica_groups=mesh['gx'=4,'gy'=8] {'gy'}, dimensions={0} | all-to-all | bytes 1048576 | tf_op jit(solution)/shard_map/all_to_all | solution.py:85
  352.3 2.4 fusion.323
  354.8 14.5 %fusion.279 = bf16[64,16,8,64]{3,0,2,1:T(8,128)(2,1)S(1)} fusion(f32[64,16,8,64]{3,0,2,1:T(8,128)S(1)} %fusion.323, f32[64,16,8,64]{3,0,2,1:T(8,128)} %copy-done.1, f32[64]{0:T(128)S(1)} %copy-done.11, f32[64,64]{1,0:T(8,128)S(1)} %copy-done), kind=kOutput, calls=%fused_computation.339 | convolution fusion | flops 437780480 | bytes 5259520 | tf_op jit(solution)/shard_map/oxyz,oq->qxyz/dot_general | solution.py:90
  369.3 1.4 fusion.290
  370.7 1.0 copy.78
  371.7 3.5 all-to-all-start.6
  375.2 9.6 %all-to-all-done.6 = bf16[8,4,64,128]{3,1,2,0:T(4,128)(2,1)S(1)} async-done(((bf16[8,4,64,128]{3,1,2,0:T(4,128)(2,1)}), bf16[8,4,64,128]{3,1,2,0:T(4,128)(2,1)S(1)}, u32[]{:S(2)}, u32[]{:S(2)}) %all-to-all-start.6) | async-done | bytes 524320 | tf_op jit(solution)/shard_map/all_to_all | solution.py:169
  385.0 1.0 fusion.294
  386.0 174.1 %while.25 = (s32[]{:T(128)}, f32[2,8,128]{2,1,0:T(8,128)}, bf16[64,64]{1,0:T(8,128)(2,1)S(1)}, bf16[2,8,64,128]{3,1,0,2:T(8,128)(2,1)}, bf16[2,8,3,128]{3,1,2,0:...) while((s32[]{:T(128)}, f32[2,8,128]{2,1,0:T(8,128)}, ...), condition=%wide.region_5.6_spmd, body=%wide.region_4.5_spmd.sunk | while | flops 1684092928 | bytes 22110176 | solution.py:65
  387.2 0.8 slice_bitcast_fusion.9
  388.1 0.9 constant_dynamic-slice_fusion.2
  389.1 2.2 multiply_convert_fusion.9
  391.3 80.4 %fusion.380 = f32[8,64,128]{2,1,0:T(8,128)S(1)} fusion(f32[8,128,128]{2,1,0:T(8,128)S(1)} %get-tuple-element.455, f32[64]{0:T(128)S(1)} %get-tuple-element.510, f32[8,128,64]{1,2,0:T(8,128)S(1)} %broadcast_multiply_fusion.5, f32[64]{0:T(128)S(1)} %get-tuple-element.458, f32[8,128,128]{2,1,0:T(8,128)S(1)} %get-tuple-element.459, ...), kind=kOutput, calls=%fused_computation.27.clone.3 | convolution fusion | flops 1669332992 | bytes 10486528 | tf_op jit(solution)/shard_map/while/body/eval_jaxpr/bcph,bcho->bop/dot_general | solution.py:52
  471.7 0.8 fusion.381
  475.0 0.9 constant_dynamic-slice_fusion.2
  476.0 2.2 multiply_convert_fusion.9
  478.3 80.4 %fusion.380 = f32[8,64,128]{2,1,0:T(8,128)S(1)} fusion(f32[8,128,128]{2,1,0:T(8,128)S(1)} %get-tuple-element.455, f32[64]{0:T(128)S(1)} %get-tuple-element.510, f32[8,128,64]{1,2,0:T(8,128)S(1)} %broadcast_multiply_fusion.5, f32[64]{0:T(128)S(1)} %get-tuple-element.458, f32[8,128,128]{2,1,0:T(8,128)S(1)} %get-tuple-element.459, ...), kind=kOutput, calls=%fused_computation.27.clone.3 | convolution fusion | flops 1669332992 | bytes 10486528 | tf_op jit(solution)/shard_map/while/body/eval_jaxpr/bcph,bcho->bop/dot_general | solution.py:52
  558.6 0.8 fusion.381
  (101 shorter events, 21.3 us)
Async XLA Ops:
  0.0 354.7 %copy-start = (f32[64,64]{1,0:T(8,128)S(1)}, f32[64,64]{1,0:T(8,128)}, u32[]{:S(2)}) copy-start(f32[64,64]{1,0:T(8,128)} %param.29) | copy-start | bytes 49156
  2.3 0.6 copy-start.7
  4.4 189.3 %all-to-all-start = ((f32[8,1,4]{2,1,0:T(1,128)}), f32[8,1,4]{2,1,0:T(1,128)}, u32[]{:S(2)}, u32[]{:S(2)}) async-start(f32[8,1,4]{2,1,0:T(1,128)} %bitcast.37), calls=%async_computation | async-start | bytes 8192 | tf_op jit(solution)/shard_map/all_to_all | solution.py:154
  11.5 179.2 %copy-start.6 = (s32[8,4]{0,1:T(4,128)S(1)}, s32[8,4]{0,1:T(4,128)}, u32[]{:S(2)}) copy-start(s32[8,4]{0,1:T(4,128)} %multiply_add_fusion) | copy-start | bytes 388
  11.5 179.2 %copy-start.8 = (s32[16]{0:T(128)S(1)}, s32[16]{0:T(128)}, u32[]{:S(2)}) copy-start(s32[16]{0:T(128)} %copy-done.7) | copy-start | bytes 196
  14.1 86.1 %copy-start.2 = (f32[2,8,64,128]{3,2,1,0:T(8,128)S(1)}, f32[2,8,64,128]{3,2,1,0:T(8,128)}, u32[]{:S(2)}) copy-start(f32[2,8,64,128]{3,2,1,0:T(8,128)} %get-tuple-element.471) | copy-start | bytes 1572868 | tf_op jit(solution)/shard_map/while
  100.2 0.8 copy-start.3
  103.6 86.1 %copy-start.2 = (f32[2,8,64,128]{3,2,1,0:T(8,128)S(1)}, f32[2,8,64,128]{3,2,1,0:T(8,128)}, u32[]{:S(2)}) copy-start(f32[2,8,64,128]{3,2,1,0:T(8,128)} %get-tuple-element.471) | copy-start | bytes 1572868 | tf_op jit(solution)/shard_map/while
  189.7 0.8 copy-start.3
  193.7 19.6 %all-to-all-start.1 = ((f32[8,4,64,128]{3,2,1,0:T(8,128)}), f32[8,4,64,128]{3,2,1,0:T(8,128)S(1)}, u32[]{:S(2)}, u32[]{:S(2)}) async-start(f32[8,4,64,128]{3,2,1,0:T(8,128)} %copy.61), calls=%async_computation.1 | async-start | bytes 2097152 | tf_op jit(solution)/shard_map/all_to_all | solution.py:147
  218.7 2.1 copy-start.1
  249.3 33.8 %all-to-all-start.3 = ((f32[4,1,32768]{2,1,0:T(1,128)}), f32[4,1,32768]{2,1,0:T(1,128)S(1)}, u32[]{:S(2)}, u32[]{:S(2)}) async-start(f32[4,1,32768]{2,1,0:T(1,128)} %reshape.241), calls=%async_computation.3 | async-start | bytes 1048576 | tf_op jit(solution)/shard_map/all_to_all | solution.py:76
  287.1 67.6 %copy-start.11 = (f32[64]{0:T(128)S(1)}, f32[64]{0:T(128)}, u32[]{:S(2)}) copy-start(f32[64]{0:T(128)} %param.30) | copy-start | bytes 772
  354.7 31.3 %copy-start.4 = (bf16[64,64]{1,0:T(8,128)(2,1)S(1)}, bf16[64,64]{1,0:T(8,128)(2,1)}, u32[]{:S(2)}) copy-start(bf16[64,64]{1,0:T(8,128)(2,1)} %param.27) | copy-start | bytes 24580
  354.7 31.3 %copy-start.12 = (f32[64]{0:T(128)S(1)}, f32[64]{0:T(128)}, u32[]{:S(2)}) copy-start(f32[64]{0:T(128)} %param.26) | copy-start | bytes 772
  371.7 13.1 %all-to-all-start.6 = ((bf16[8,4,64,128]{3,1,2,0:T(4,128)(2,1)}), bf16[8,4,64,128]{3,1,2,0:T(4,128)(2,1)S(1)}, u32[]{:S(2)}, u32[]{:S(2)}) async-start(bf16[8,4,64,128]{3,1,2,0:T(4,128)(2,1)} %copy.78), calls=%async_computation.6 | async-start | bytes 1048576 | tf_op jit(solution)/shard_map/all_to_all | solution.py:169
  391.3 80.4 %copy-start.13 = (f32[64]{0:T(128)S(1)}, f32[64]{0:T(128)}, u32[]{:S(2)}) copy-start(f32[64]{0:T(128)} %get-tuple-element.511) | copy-start | bytes 772 | tf_op jit(solution)/shard_map/while
  391.3 81.2 %copy-start.9 = (f32[2,8,128]{2,1,0:T(8,128)S(1)}, f32[2,8,128]{2,1,0:T(8,128)}, u32[]{:S(2)}) copy-start(f32[2,8,128]{2,1,0:T(8,128)} %get-tuple-element.496) | copy-start | bytes 24580 | tf_op jit(solution)/shard_map/while
  391.3 81.8 %copy-start.5 = (bf16[64,64]{1,0:T(8,128)(2,1)S(1)}, bf16[64,64]{1,0:T(8,128)(2,1)}, u32[]{:S(2)}) copy-start(bf16[64,64]{1,0:T(8,128)(2,1)} %get-tuple-element.525) | copy-start | bytes 24580 | tf_op jit(solution)/shard_map/while
  472.5 0.6 copy-start.10
  478.2 80.4 %copy-start.13 = (f32[64]{0:T(128)S(1)}, f32[64]{0:T(128)}, u32[]{:S(2)}) copy-start(f32[64]{0:T(128)} %get-tuple-element.511) | copy-start | bytes 772 | tf_op jit(solution)/shard_map/while
  478.2 81.2 %copy-start.9 = (f32[2,8,128]{2,1,0:T(8,128)S(1)}, f32[2,8,128]{2,1,0:T(8,128)}, u32[]{:S(2)}) copy-start(f32[2,8,128]{2,1,0:T(8,128)} %get-tuple-element.496) | copy-start | bytes 24580 | tf_op jit(solution)/shard_map/while
  478.3 81.8 %copy-start.5 = (bf16[64,64]{1,0:T(8,128)(2,1)S(1)}, bf16[64,64]{1,0:T(8,128)(2,1)}, u32[]{:S(2)}) copy-start(bf16[64,64]{1,0:T(8,128)(2,1)} %get-tuple-element.525) | copy-start | bytes 24580 | tf_op jit(solution)/shard_map/while
  559.5 0.6 copy-start.10
where the time goes:
time: 571 us; the launch traced here: 560 us
  matrix products  408 us (71%)
  local copies, waits for them, and re-layouts  56.7 us (10%)
  blocking collectives  37.1 us (6%)
  waiting for transfers between devices  22.9 us (4%)
  starting transfers between devices  17.8 us (3%)
  other arithmetic  16.8 us (3%)
    dot_general x2, matrix products, encode(): jnp.einsum('bcph,bop->bcho', weighted, feats, preferred_element_type=jnp....  172 us
    dot_general x2, matrix products, decode(): jnp.einsum('bcph,bcho->bop', weighted, folded, preferred_element_type=jnp...  161 us
    dot_general x1, matrix products, fourier(): jnp.einsum('ojlk,jlkoq->qjlk', spectrum, mode_weight, precision=highest)  32.6 us
    reshape x1, local copies, waits for them, and re-layouts, fourier(): spec_weight.reshape(spec_weight.shape[:3] + (channels, channels))  28.9 us
    dot_general x1, matrix products, fourier(): jnp.einsum('oxyz,oq->qxyz', pencil, local_weight, precision=highest)  14.5 us
    all_to_all x1, waiting for transfers between devices, local(): lax.all_to_all(send_terms.reshape(cols_count, capacity, channels, tile_ce...  13.3 us
    all_to_all x1, blocking collectives, fourier(): lax.all_to_all(returned.astype(jnp.bfloat16), 'gx', split_axis=1, concat_...  12.7 us
    all_to_all x1, blocking collectives, fourier(): lax.all_to_all(returned.astype(jnp.bfloat16), 'gy', split_axis=2, concat_...  12.3 us
  transfers between devices with their start and end apart: 4, of which 2 were waited for; matrix products, arithmetic and copies ran while one was open for 38% of the time, Pallas kernels for 0%

commit v1 on v0

--- a/solution.py
+++ b/solution.py
@@ -82,8 +82,14 @@
         returned.astype(jnp.bfloat16), "gx", split_axis=1, concat_axis=2, tiled=True
     ).astype(returned.dtype)
     returned = jnp.einsum("oxlk,ly->oxyk", returned, table, precision=highest)
-    returned = lax.all_to_all(
-        returned.astype(jnp.bfloat16), "gy", split_axis=2, concat_axis=3, tiled=True
+    returned = jnp.concatenate(
+        lax.all_to_all(
+            jnp.stack(jnp.split(returned.astype(jnp.bfloat16), lax.axis_size("gy"), axis=2)),
+            "gy",
+            0,
+            0,
+        ),
+        axis=3,
     ).astype(returned.dtype)
     returned = jnp.einsum("oxyk,kz->oxyz", returned, table, precision=highest)
     local_term = (

time: 571 us -> 570 us (level)
  no operation moved by 1% of the time
where the time goes in v1:
time: 570 us; the launch traced here: 560 us
  matrix products  408 us (72%)
  local copies, waits for them, and re-layouts  55.9 us (10%)
  blocking collectives  37.2 us (7%)
  waiting for transfers between devices  22.9 us (4%)
  starting transfers between devices  17.8 us (3%)
  other arithmetic  16.8 us (3%)
    dot_general x2, matrix products, encode(): jnp.einsum('bcph,bop->bcho', weighted, feats, preferred_element_type=jnp....  172 us
    dot_general x2, matrix products, decode(): jnp.einsum('bcph,bcho->bop', weighted, folded, preferred_element_type=jnp...  161 us
    dot_general x1, matrix products, fourier(): jnp.einsum('ojlk,jlkoq->qjlk', spectrum, mode_weight, precision=highest)  32.6 us
    reshape x1, local copies, waits for them, and re-layouts, fourier(): spec_weight.reshape(spec_weight.shape[:3] + (channels, channels))  28.9 us
    dot_general x1, matrix products, fourier(): jnp.einsum('oxyz,oq->qxyz', pencil, local_weight, precision=highest)  14.5 us
    all_to_all x1, waiting for transfers between devices, local(): lax.all_to_all(send_terms.reshape(cols_count, capacity, channels, tile_ce...  13.3 us
    all_to_all x1, blocking collectives, fourier(): lax.all_to_all(returned.astype(jnp.bfloat16), 'gx', split_axis=1, concat_...  12.7 us
    all_to_all x1, blocking collectives, fourier(): lax.all_to_all(jnp.stack(jnp.split(returned.astype(jnp.bfloat16), lax.axi...  12.3 us
  transfers between devices with their start and end apart: 4, of which 2 were waited for; matrix products, arithmetic and copies ran while one was open for 38% of the time, Pallas kernels for 0%

profile of v1, /device:TPU:0, one launch (start us, length us, event | category | flops | bytes accessed | tf_op | source)
XLA Modules:
  0.0 559.7 jit_solution(15994533511022582742)
XLA Ops:
  0.8 0.8 select_reduce_fusion
  2.8 0.8 convolution_bitcast_fusion.2
  4.4 5.2 all-to-all-start
  10.1 1.3 copy.59
  11.5 179.2 %while.24 = (s32[]{:T(128)}, f32[2,8,64,128]{3,2,1,0:T(8,128)}, bf16[2,8,3,128]{3,1,2,0:T(8,128)(2,1)}, f32[3,64]{1,0:T(4,128)}, f32[64]{0:T(128)}, /*index=5*/b...) while((s32[]{:T(128)}, f32[2,8,64,128]{3,2,1,0:T(8,128)}, bf16[2,8,3,128]{3,1,2,0:T(8,128)(2,1)}, ...), condition=%wide.region_3.4_spmd, body=%wide.region_2.3_spmd.sunk | while | flops 1678981120 | bytes 9416085 | solution.py:65
  12.5 0.8 slice_bitcast_fusion.16
  14.1 85.9 %multiply_reduce_fusion.2 = f32[64,8,128]{0,2,1:T(8,128)S(1)} fusion(f32[64,64]{0,1:T(8,128)S(1)} %bitcast_convert_fusion.6, f32[8,128,128]{2,1,0:T(8,128)S(1)} %get-tuple-element.435, f32[64]{0:T(128)} %get-tuple-element.482, f32[8,128,64]{1,2,0:T(8,128)S(1)} %broadcast_multiply_fusion.4, f32[64]{0:T(128)S(1)} %get-tuple-element.438, ...), kind=kOutput, calls=%fused_computation.219.clone.3 | convolution fusion | flops 1677656064 | bytes 2246144 | tf_op jit(solution)/shard_map/while/body/eval_jaxpr/bcph,bop->bcho/dot_general | solution.py:41
  102.0 0.8 slice_bitcast_fusion.16
  103.6 85.9 %multiply_reduce_fusion.2 = f32[64,8,128]{0,2,1:T(8,128)S(1)} fusion(f32[64,64]{0,1:T(8,128)S(1)} %bitcast_convert_fusion.6, f32[8,128,128]{2,1,0:T(8,128)S(1)} %get-tuple-element.435, f32[64]{0:T(128)} %get-tuple-element.482, f32[8,128,64]{1,2,0:T(8,128)S(1)} %broadcast_multiply_fusion.4, f32[64]{0:T(128)S(1)} %get-tuple-element.438, ...), kind=kOutput, calls=%fused_computation.219.clone.3 | convolution fusion | flops 1677656064 | bytes 2246144 | tf_op jit(solution)/shard_map/while/body/eval_jaxpr/bcph,bop->bcho/dot_general | solution.py:41
  190.7 1.8 fusion.302
  192.5 1.2 copy.61
  193.7 4.2 all-to-all-start.1
  198.6 1.3 reduce.5
  200.0 13.3 %all-to-all-done.1 = f32[8,4,64,128]{3,2,1,0:T(8,128)S(1)} async-done(((f32[8,4,64,128]{3,2,1,0:T(8,128)}), f32[8,4,64,128]{3,2,1,0:T(8,128)S(1)}, u32[]{:S(2)}, u32[]{:S(2)}) %all-to-all-start.1) | async-done | bytes 1048608 | tf_op jit(solution)/shard_map/all_to_all | solution.py:153
  213.3 1.8 copy.62
  215.1 3.5 fusion.319
  218.7 2.1 copy-done.1
  220.7 11.4 %convolution_convert_fusion.1 = bf16[64,16,8,32]{0,3,2,1:T(8,128)(2,1)S(1)} fusion(f32[64,16,8,64]{3,0,2,1:T(8,128)S(1)} %fusion.319, f32[16,64]{1,0:T(8,128)S(1)} %get-tuple-element.319, f32[16,64]{1,0:T(8,128)S(1)} %get-tuple-element.318), kind=kOutput, calls=%fused_computation.359 | convolution fusion | flops 201592832 | bytes 2629632 | tf_op jit(solution)/shard_map/oxyz,kz->oxyk/dot_general | solution.py:71
  232.6 0.9 reshape.247
  233.5 12.1 %all_to_all.78 = bf16[8,2,16384]{2,1,0:T(2,128)(2,1)S(1)} all-to-all(bf16[8,2,16384]{2,1,0:T(2,128)(2,1)S(1)} %reshape.247), channel_id=1, replica_groups=mesh['gx'=4,'gy'=8] {'gy'}, dimensions={0} | all-to-all | bytes 1048576 | tf_op jit(solution)/shard_map/all_to_all | solution.py:72
  247.6 1.8 reshape.249
  249.3 4.9 all-to-all-start.3
  254.3 28.9 %reshape.210 = f32[32,8,4,64,64]{4,3,2,1,0:T(8,128)} reshape(f32[32,8,4,4096]{3,2,1,0:T(4,128)} %param.28) | data formatting | bytes 33554432 | tf_op jit(solution)/shard_map/reshape | solution.py:78
  283.7 2.1 reduce.8
  287.3 1.2 convolution_bitcast_fusion.1
  288.5 32.6 %fusion.305 = f32[32,8,4,1,64]{4,3,2,1,0:T(1,128)S(1)} fusion(f32[32,8,4,64,64]{4,3,2,1,0:T(8,128)} %reshape.210, f32[64,32,8,4,1]{0,1,3,2,4:T(8,128)S(1)} %convolution_bitcast_fusion.1), kind=kOutput, calls=%fused_computation.380 | convolution fusion | flops 50331648 | bytes 17301504 | tf_op jit(solution)/shard_map/ojlk,jlkoq->qjlk/dot_general | solution.py:79
  321.2 1.2 fusion.293
  323.2 12.7 %all_to_all.79 = bf16[4,2,16384]{2,1,0:T(2,128)(2,1)S(1)} all-to-all(bf16[4,2,16384]{2,1,0:T(2,128)(2,1)S(1)} %reshape.251), channel_id=1, replica_groups=mesh['gx'=4,'gy'=8] {'gx'}, dimensions={0} | all-to-all | bytes 524288 | tf_op jit(solution)/shard_map/all_to_all | solution.py:81
  336.3 1.0 fusion.289
  338.4 12.3 %all_to_all.80 = bf16[8,2,16384]{2,1,0:T(2,128)(2,1)S(1)} all-to-all(bf16[8,2,16384]{2,1,0:T(2,128)(2,1)S(1)} %reshape.253), channel_id=1, replica_groups=mesh['gx'=4,'gy'=8] {'gy'}, dimensions={0} | all-to-all | bytes 1048576 | tf_op jit(solution)/shard_map/all_to_all | solution.py:86
  351.6 2.4 fusion.297
  354.0 14.5 %fusion.279 = bf16[64,16,8,64]{3,0,2,1:T(8,128)(2,1)S(1)} fusion(f32[64,16,8,64]{3,0,2,1:T(8,128)S(1)} %fusion.297, f32[64,16,8,64]{3,0,2,1:T(8,128)} %copy-done.1, f32[64]{0:T(128)S(1)} %copy-done.11, f32[64,64]{1,0:T(8,128)S(1)} %copy-done), kind=kOutput, calls=%fused_computation.339 | convolution fusion | flops 437780480 | bytes 5259520 | tf_op jit(solution)/shard_map/oxyz,oq->qxyz/dot_general | solution.py:96
  368.6 1.4 fusion.290
  369.9 1.0 copy.78
  370.9 3.5 all-to-all-start.6
  374.5 9.6 %all-to-all-done.6 = bf16[8,4,64,128]{3,1,2,0:T(4,128)(2,1)S(1)} async-done(((bf16[8,4,64,128]{3,1,2,0:T(4,128)(2,1)}), bf16[8,4,64,128]{3,1,2,0:T(4,128)(2,1)S(1)}, u32[]{:S(2)}, u32[]{:S(2)}) %all-to-all-start.6) | async-done | bytes 524320 | tf_op jit(solution)/shard_map/all_to_all | solution.py:175
  384.3 1.0 fusion.294
  385.3 174.1 %while.25 = (s32[]{:T(128)}, f32[2,8,128]{2,1,0:T(8,128)}, bf16[64,64]{1,0:T(8,128)(2,1)S(1)}, bf16[2,8,64,128]{3,1,0,2:T(8,128)(2,1)}, bf16[2,8,3,128]{3,1,2,0:...) while((s32[]{:T(128)}, f32[2,8,128]{2,1,0:T(8,128)}, ...), condition=%wide.region_5.6_spmd, body=%wide.region_4.5_spmd.sunk | while | flops 1684092928 | bytes 22110176 | solution.py:65
  386.5 0.8 slice_bitcast_fusion.17
  387.3 0.9 constant_dynamic-slice_fusion.2
  388.3 2.2 multiply_convert_fusion.9
  390.6 80.4 %fusion.388 = f32[8,64,128]{2,1,0:T(8,128)S(1)} fusion(f32[8,128,128]{2,1,0:T(8,128)S(1)} %get-tuple-element.455, f32[64]{0:T(128)S(1)} %get-tuple-element.510, f32[8,128,64]{1,2,0:T(8,128)S(1)} %broadcast_multiply_fusion.5, f32[64]{0:T(128)S(1)} %get-tuple-element.458, f32[8,128,128]{2,1,0:T(8,128)S(1)} %get-tuple-element.459, ...), kind=kOutput, calls=%fused_computation.27.clone.3 | convolution fusion | flops 1669332992 | bytes 10486528 | tf_op jit(solution)/shard_map/while/body/eval_jaxpr/bcph,bcho->bop/dot_general | solution.py:52
  471.0 0.8 fusion.389
  473.4 0.8 slice_bitcast_fusion.17
  474.3 0.9 constant_dynamic-slice_fusion.2
  475.3 2.2 multiply_convert_fusion.9
  477.5 80.4 %fusion.388 = f32[8,64,128]{2,1,0:T(8,128)S(1)} fusion(f32[8,128,128]{2,1,0:T(8,128)S(1)} %get-tuple-element.455, f32[64]{0:T(128)S(1)} %get-tuple-element.510, f32[8,128,64]{1,2,0:T(8,128)S(1)} %broadcast_multiply_fusion.5, f32[64]{0:T(128)S(1)} %get-tuple-element.458, f32[8,128,128]{2,1,0:T(8,128)S(1)} %get-tuple-element.459, ...), kind=kOutput, calls=%fused_computation.27.clone.3 | convolution fusion | flops 1669332992 | bytes 10486528 | tf_op jit(solution)/shard_map/while/body/eval_jaxpr/bcph,bcho->bop/dot_general | solution.py:52
  557.9 0.8 fusion.389
  (109 shorter events, 20.6 us)
Async XLA Ops:
  0.0 354.0 %copy-start = (f32[64,64]{1,0:T(8,128)S(1)}, f32[64,64]{1,0:T(8,128)}, u32[]{:S(2)}) copy-start(f32[64,64]{1,0:T(8,128)} %param.29) | copy-start | bytes 49156
  2.3 0.6 copy-start.7
  4.4 189.3 %all-to-all-start = ((f32[8,1,4]{2,1,0:T(1,128)}), f32[8,1,4]{2,1,0:T(1,128)}, u32[]{:S(2)}, u32[]{:S(2)}) async-start(f32[8,1,4]{2,1,0:T(1,128)} %bitcast.37), calls=%async_computation | async-start | bytes 8192 | tf_op jit(solution)/shard_map/all_to_all | solution.py:160
  11.5 179.2 %copy-start.6 = (s32[8,4]{0,1:T(4,128)S(1)}, s32[8,4]{0,1:T(4,128)}, u32[]{:S(2)}) copy-start(s32[8,4]{0,1:T(4,128)} %multiply_add_fusion) | copy-start | bytes 388
  11.5 179.2 %copy-start.8 = (s32[16]{0:T(128)S(1)}, s32[16]{0:T(128)}, u32[]{:S(2)}) copy-start(s32[16]{0:T(128)} %copy-done.7) | copy-start | bytes 196
  14.1 86.1 %copy-start.2 = (f32[2,8,64,128]{3,2,1,0:T(8,128)S(1)}, f32[2,8,64,128]{3,2,1,0:T(8,128)}, u32[]{:S(2)}) copy-start(f32[2,8,64,128]{3,2,1,0:T(8,128)} %get-tuple-element.471) | copy-start | bytes 1572868 | tf_op jit(solution)/shard_map/while
  100.2 0.8 copy-start.3
  103.6 86.1 %copy-start.2 = (f32[2,8,64,128]{3,2,1,0:T(8,128)S(1)}, f32[2,8,64,128]{3,2,1,0:T(8,128)}, u32[]{:S(2)}) copy-start(f32[2,8,64,128]{3,2,1,0:T(8,128)} %get-tuple-element.471) | copy-start | bytes 1572868 | tf_op jit(solution)/shard_map/while
  189.7 0.8 copy-start.3
  193.7 19.6 %all-to-all-start.1 = ((f32[8,4,64,128]{3,2,1,0:T(8,128)}), f32[8,4,64,128]{3,2,1,0:T(8,128)S(1)}, u32[]{:S(2)}, u32[]{:S(2)}) async-start(f32[8,4,64,128]{3,2,1,0:T(8,128)} %copy.61), calls=%async_computation.1 | async-start | bytes 2097152 | tf_op jit(solution)/shard_map/all_to_all | solution.py:153
  218.7 2.1 copy-start.1
  249.3 33.8 %all-to-all-start.3 = ((f32[4,1,32768]{2,1,0:T(1,128)}), f32[4,1,32768]{2,1,0:T(1,128)S(1)}, u32[]{:S(2)}, u32[]{:S(2)}) async-start(f32[4,1,32768]{2,1,0:T(1,128)} %reshape.249), calls=%async_computation.3 | async-start | bytes 1048576 | tf_op jit(solution)/shard_map/all_to_all | solution.py:76
  287.3 66.7 %copy-start.11 = (f32[64]{0:T(128)S(1)}, f32[64]{0:T(128)}, u32[]{:S(2)}) copy-start(f32[64]{0:T(128)} %param.30) | copy-start | bytes 772
  354.0 31.3 %copy-start.4 = (bf16[64,64]{1,0:T(8,128)(2,1)S(1)}, bf16[64,64]{1,0:T(8,128)(2,1)}, u32[]{:S(2)}) copy-start(bf16[64,64]{1,0:T(8,128)(2,1)} %param.27) | copy-start | bytes 24580
  354.0 31.3 %copy-start.12 = (f32[64]{0:T(128)S(1)}, f32[64]{0:T(128)}, u32[]{:S(2)}) copy-start(f32[64]{0:T(128)} %param.26) | copy-start | bytes 772
  370.9 13.1 %all-to-all-start.6 = ((bf16[8,4,64,128]{3,1,2,0:T(4,128)(2,1)}), bf16[8,4,64,128]{3,1,2,0:T(4,128)(2,1)S(1)}, u32[]{:S(2)}, u32[]{:S(2)}) async-start(bf16[8,4,64,128]{3,1,2,0:T(4,128)(2,1)} %copy.78), calls=%async_computation.6 | async-start | bytes 1048576 | tf_op jit(solution)/shard_map/all_to_all | solution.py:175
  390.5 80.4 %copy-start.13 = (f32[64]{0:T(128)S(1)}, f32[64]{0:T(128)}, u32[]{:S(2)}) copy-start(f32[64]{0:T(128)} %get-tuple-element.511) | copy-start | bytes 772 | tf_op jit(solution)/shard_map/while
  390.6 81.2 %copy-start.9 = (f32[2,8,128]{2,1,0:T(8,128)S(1)}, f32[2,8,128]{2,1,0:T(8,128)}, u32[]{:S(2)}) copy-start(f32[2,8,128]{2,1,0:T(8,128)} %get-tuple-element.496) | copy-start | bytes 24580 | tf_op jit(solution)/shard_map/while
  390.6 81.8 %copy-start.5 = (bf16[64,64]{1,0:T(8,128)(2,1)S(1)}, bf16[64,64]{1,0:T(8,128)(2,1)}, u32[]{:S(2)}) copy-start(bf16[64,64]{1,0:T(8,128)(2,1)} %get-tuple-element.525) | copy-start | bytes 24580 | tf_op jit(solution)/shard_map/while
  471.8 0.6 copy-start.10
  477.5 80.4 %copy-start.13 = (f32[64]{0:T(128)S(1)}, f32[64]{0:T(128)}, u32[]{:S(2)}) copy-start(f32[64]{0:T(128)} %get-tuple-element.511) | copy-start | bytes 772 | tf_op jit(solution)/shard_map/while
  477.5 81.2 %copy-start.9 = (f32[2,8,128]{2,1,0:T(8,128)S(1)}, f32[2,8,128]{2,1,0:T(8,128)}, u32[]{:S(2)}) copy-start(f32[2,8,128]{2,1,0:T(8,128)} %get-tuple-element.496) | copy-start | bytes 24580 | tf_op jit(solution)/shard_map/while
  477.5 81.8 %copy-start.5 = (bf16[64,64]{1,0:T(8,128)(2,1)S(1)}, bf16[64,64]{1,0:T(8,128)(2,1)}, u32[]{:S(2)}) copy-start(bf16[64,64]{1,0:T(8,128)(2,1)} %get-tuple-element.525) | copy-start | bytes 24580 | tf_op jit(solution)/shard_map/while
  558.7 0.6 copy-start.10
